TPU v7x, 256 devices: a whole 4x4x8 slice. The times are simulated.
256 devices in a mesh: dp: 4 (over y), expert: 32 (over x, z), tensor: 2 (over core).
Axes of the slice: x: 4, y: 4, z: 8, core: 2. Of those that a mesh axis runs over, the one named last changes fastest.
Arguments:
- tokens: bfloat16 [16384, 4096], P(('dp', 'expert')), may hold values from -6 to 6
- cotangent: bfloat16 [16384, 4096], P(('dp', 'expert')), may hold values from -6 to 6
- routes: int32 [16384, 1], P(('dp', 'expert')), may hold values from 0 to 31; in each aligned block of 128 rows (0 to 127, 128 to 255, ...) at most 6 rows name the same one
- cluster: int32 [32, 512], replicated, may hold values from -1 to 14783, as said below
- w_gate: bfloat16 [14784, 4096], P(('expert', 'tensor'), 'dp'), may hold values from -0.09375 to 0.09375
- w_up: bfloat16 [14784, 4096], P(('expert', 'tensor'), 'dp'), may hold values from -0.09375 to 0.09375
- w_down: bfloat16 [14784, 4096], P(('expert', 'tensor'), 'dp'), may hold values from -0.25 to 0.25
Outputs:
- layer_out: bfloat16 [16384, 4096], P(('dp', 'expert'))
- grad_tokens: bfloat16 [16384, 4096], P(('dp', 'expert'))
Inputs may be any that keep to these rules, and one draw needn't show every extreme that they name: `routes`: in each aligned block of 128 rows no expert is named more than 6 times, and some block names one expert exactly 6 times; every expert is named somewhere. `cluster`: every neuron appears exactly once and each expert has 462 live slots. Slot j = q * 256 + s * 4 + k (k below 4) holds -1 or a neuron of source shard s, that is a row from s * 231 to (s + 1) * 231 - 1; shard s fills exactly 4 such slots of some experts' halves and fewer of others.
All inputs are finite; a program needn't handle non-finite values.
Results may differ from a plain program's by a relative error of at most 0.0059.
Values may be sent and summed in bfloat16 or wider, within the bound.
A program may use at most 128 MiB of HBM per device.

v0:
```python
import jax
import jax.numpy as jnp
from jax import lax
from jax.sharding import PartitionSpec as P


def expert_math(x_rows, dy_rows, gate_w, up_w, down_w):
    contract = (((1,), (1,)), ((), ()))
    pre_gate = lax.dot_general(x_rows, gate_w, contract, preferred_element_type=jnp.float32)
    pre_up = lax.dot_general(x_rows, up_w, contract, preferred_element_type=jnp.float32)
    sig_gate = jax.nn.sigmoid(pre_gate)
    hidden = (pre_gate * sig_gate * pre_up).astype(jnp.bfloat16)
    out_part = jnp.dot(hidden, down_w, preferred_element_type=jnp.float32)
    grad_hidden = lax.dot_general(dy_rows, down_w, contract, preferred_element_type=jnp.float32)
    grad_gate = (grad_hidden * pre_up * sig_gate * (1.0 + pre_gate * (1.0 - sig_gate))).astype(
        jnp.bfloat16
    )
    grad_up = (grad_hidden * pre_gate * sig_gate).astype(jnp.bfloat16)
    grad_part = jnp.dot(grad_gate, gate_w, preferred_element_type=jnp.float32)
    grad_part = grad_part + jnp.dot(grad_up, up_w, preferred_element_type=jnp.float32)
    return (out_part, grad_part)


def to_tokens(dispatch_table, returned):
    contract = (((0,), (0,)), ((), ()))
    merged = lax.dot_general(dispatch_table, returned, contract, preferred_element_type=jnp.float32)
    return merged.astype(jnp.bfloat16)


def per_device(tokens, cotangent, routes, cluster, w_gate, w_up, w_down):
    shards = lax.axis_size(("expert", "tensor"))
    source = lax.axis_index(("expert", "tensor"))
    halves = lax.axis_size("tensor")
    rows_dev = w_gate.shape[0]
    width_part = w_gate.shape[1]
    n_experts = cluster.shape[0]
    half_slots = cluster.shape[1] // halves
    per_shard = half_slots // shards
    picks = cluster.reshape(shards, shards, per_shard)
    my_picks = lax.dynamic_index_in_dim(picks, source, 1, keepdims=False)
    is_live = (my_picks >= 0)[:, :, None]
    row_index = jnp.clip(my_picks - source * rows_dev, 0, rows_dev - 1).reshape(-1)

    def select_rows(weight):
        chosen = jnp.take(weight, row_index, axis=0).reshape(shards, per_shard, width_part)
        return jnp.where(is_live, chosen, jnp.zeros((), jnp.bfloat16))

    sent_gate = select_rows(w_gate)
    sent_up = select_rows(w_up)
    sent_down = select_rows(w_down)
    received = (
        lax.all_to_all(sent_gate, ("expert", "tensor"), split_axis=0, concat_axis=0, tiled=True),
        lax.all_to_all(sent_up, ("expert", "tensor"), split_axis=0, concat_axis=0, tiled=True),
        lax.all_to_all(sent_down, ("expert", "tensor"), split_axis=0, concat_axis=0, tiled=True),
    )
    part_gate = received[0].reshape(half_slots, width_part)
    part_up = received[1].reshape(half_slots, width_part)
    part_down = received[2].reshape(half_slots, width_part)
    gate_w, up_w, down_w = (
        lax.all_gather(part_gate, "dp", axis=1, tiled=True),
        lax.all_gather(part_up, "dp", axis=1, tiled=True),
        lax.all_gather(part_down, "dp", axis=1, tiled=True),
    )
    tok_count = tokens.shape[0]
    width = tokens.shape[1]
    capacity = max(2, 3 * tok_count // (2 * n_experts))
    expert_of = routes[:, 0]
    onehot = (expert_of[:, None] == jnp.arange(n_experts, dtype=jnp.int32)[None, :]).astype(
        jnp.int32
    )
    position = jnp.sum((jnp.cumsum(onehot, axis=0) - 1) * onehot, axis=1)
    slot_id = expert_of * capacity + position
    buffer_rows = n_experts * capacity
    dispatch_table = (slot_id[None, :] == jnp.arange(buffer_rows, dtype=jnp.int32)[:, None]).astype(
        jnp.bfloat16
    )
    sent_tokens = jnp.dot(dispatch_table, tokens, preferred_element_type=jnp.float32).astype(
        jnp.bfloat16
    )
    sent_grads = jnp.dot(dispatch_table, cotangent, preferred_element_type=jnp.float32).astype(
        jnp.bfloat16
    )
    sent_tokens = sent_tokens.reshape(n_experts, capacity, width)
    sent_grads = sent_grads.reshape(n_experts, capacity, width)
    x_rows, dy_rows = (
        lax.all_to_all(sent_tokens, "expert", split_axis=0, concat_axis=0, tiled=True),
        lax.all_to_all(sent_grads, "expert", split_axis=0, concat_axis=0, tiled=True),
    )
    x_rows = x_rows.reshape(buffer_rows, width)
    dy_rows = dy_rows.reshape(buffer_rows, width)
    out_part, grad_part = expert_math(x_rows, dy_rows, gate_w, up_w, down_w)
    out_total, grad_total = (
        lax.psum(out_part.astype(jnp.bfloat16), "tensor").astype(jnp.float32),
        lax.psum(grad_part.astype(jnp.bfloat16), "tensor").astype(jnp.float32),
    )
    out_back = out_total.astype(jnp.bfloat16).reshape(n_experts, capacity, width)
    grad_back = grad_total.astype(jnp.bfloat16).reshape(n_experts, capacity, width)
    out_home, grad_home = (
        lax.all_to_all(out_back, "expert", split_axis=0, concat_axis=0, tiled=True),
        lax.all_to_all(grad_back, "expert", split_axis=0, concat_axis=0, tiled=True),
    )
    layer_out = to_tokens(dispatch_table, out_home.reshape(buffer_rows, width))
    grad_out = to_tokens(dispatch_table, grad_home.reshape(buffer_rows, width))
    return (layer_out, grad_out)


def solution(mesh):
    in_specs = (
        P(("dp", "expert"), None),
        P(("dp", "expert"), None),
        P(("dp", "expert"), None),
        P(),
        P(("expert", "tensor"), "dp"),
        P(("expert", "tensor"), "dp"),
        P(("expert", "tensor"), "dp"),
    )
    out_specs = (P(("dp", "expert"), None), P(("dp", "expert"), None))
    return jax.shard_map(
        per_device, mesh=mesh, in_specs=in_specs, out_specs=out_specs, check_vma=False
    )
```

profile of v0, /device:TPU:1, one launch (start us, length us, event | category | flops | bytes accessed | tf_op | source)
XLA Modules:
  0.0 398.1 jit_solution(12827030748125717952)
XLA Ops:
  7.2 0.0 copy-start
  7.2 0.0 all-gather.4.cloned.1.call-start
  7.2 4.5 %reshape.78 = s32[64,64,4]{2,1,0:T(8,128)} reshape(s32[32,512]{1,0:T(8,128)} %param.12) | data formatting | bytes 131072 | tf_op jit(solution)/shard_map/reshape | solution.py:39
  11.7 1.0 constant_dynamic-slice_fusion
  12.7 0.1 copy.14
  12.8 0.1 copy.13
  12.9 0.1 min.12
  13.0 0.1 copy.12
  13.2 1.2 gather_fusion.2
  14.3 1.2 gather_fusion.1
  15.5 2.0 gather_fusion
  17.5 2.4 broadcast_select_fusion.2
  19.9 1.3 reshape.79
  21.2 1.2 reshape.81
  22.4 0.2 reshape.83
  22.6 1.6 broadcast_select_fusion.5
  24.2 30.0 %all_to_all.35 = bf16[64,4,1024]{2,1,0:T(4,128)(2,1)S(1)} all-to-all(bf16[64,4,1024]{2,1,0:T(4,128)(2,1)S(1)} %get-tuple-element.5), channel_id=1, replica_groups=mesh['dp'=4,'expert'=32,'tensor'=2] {'expert','tensor'}, dimensions={0} | all-to-all | bytes 1048576 | tf_op jit(solution)/shard_map/all_to_all | solution.py:52
  54.3 0.9 reshape.80
  55.2 0.0 all-gather.4.cloned.1.call-update
  55.2 23.5 %all_to_all.36 = bf16[64,4,1024]{2,1,0:T(4,128)(2,1)} all-to-all(bf16[64,4,1024]{2,1,0:T(4,128)(2,1)S(1)} %get-tuple-element.6), channel_id=1, replica_groups=mesh['dp'=4,'expert'=32,'tensor'=2] {'expert','tensor'}, dimensions={0} | all-to-all | bytes 1048576 | tf_op jit(solution)/shard_map/all_to_all | solution.py:53
  78.7 6.3 %all-to-all-start.3 = ((bf16[64,4,1024]{2,1,0:T(4,128)(2,1)}), bf16[64,4,1024]{2,1,0:T(4,128)(2,1)S(1)}, u32[]{:S(2)}, u32[]{:S(2)}) async-start(bf16[64,4,1024]{2,1,0:T(4,128)(2,1)} %get-tuple-element.7), calls=%async_computation.3 | async-start | bytes 1048576 | tf_op jit(solution)/shard_map/all_to_all | solution.py:54
  85.0 0.1 fusion.5
  85.1 0.2 reduce_window_sum.11
  85.3 0.2 select_reduce_fusion
  85.5 0.6 convolution_convert_fusion
  86.1 1.6 reshape.87
  87.7 14.6 %all-to-all-done.3 = bf16[64,4,1024]{2,1,0:T(4,128)(2,1)S(1)} async-done(((bf16[64,4,1024]{2,1,0:T(4,128)(2,1)}), bf16[64,4,1024]{2,1,0:T(4,128)(2,1)S(1)}, u32[]{:S(2)}, u32[]{:S(2)}) %all-to-all-start.3) | async-done | bytes 524320 | tf_op jit(solution)/shard_map/all_to_all | solution.py:54
  102.3 0.8 copy-done.7
  103.1 5.2 %all-to-all-start.5 = ((bf16[32,6,4096]{2,1,0:T(8,128)(2,1)}), bf16[32,6,4096]{2,1,0:T(8,128)(2,1)S(1)}, u32[]{:S(2)}, u32[]{:S(2)}) async-start(bf16[32,6,4096]{2,1,0:T(8,128)(2,1)} %reshape.87), calls=%async_computation.5 | async-start | bytes 4194304 | tf_op jit(solution)/shard_map/all_to_all | solution.py:87
  108.3 0.0 all-gather.6.cloned.1.call-start
  108.3 2.0 reshape.82
  110.4 0.0 all-gather.6.cloned.1.call-update
  110.4 3.0 convolution_convert_fusion.2
  113.4 3.6 reshape.76
  116.9 40.4 %all-to-all-done.5 = bf16[32,6,4096]{2,1,0:T(8,128)(2,1)S(1)} async-done(((bf16[32,6,4096]{2,1,0:T(8,128)(2,1)}), bf16[32,6,4096]{2,1,0:T(8,128)(2,1)S(1)}, u32[]{:S(2)}, u32[]{:S(2)}) %all-to-all-start.5) | async-done | bytes 1572896 | tf_op jit(solution)/shard_map/all_to_all | solution.py:87
  157.3 7.1 %all-to-all-start = ((bf16[32,6,4096]{2,1,0:T(8,128)(2,1)}), bf16[32,6,4096]{2,1,0:T(8,128)(2,1)}, u32[]{:S(2)}, u32[]{:S(2)}) async-start(bf16[32,6,4096]{2,1,0:T(8,128)(2,1)} %reshape.76), calls=%async_computation | async-start | bytes 4194304 | tf_op jit(solution)/shard_map/all_to_all | solution.py:86
  164.4 0.0 all-gather.8.cloned.1.call-start
  164.4 2.0 reshape.84
  166.4 0.0 all-gather.8.cloned.1.call-update
  166.4 0.2 all-reduce.3.cloned.1.call-start
  166.6 1.4 reshape.88
  168.1 45.0 %all-to-all-done = bf16[32,6,4096]{2,1,0:T(8,128)(2,1)} async-done(((bf16[32,6,4096]{2,1,0:T(8,128)(2,1)}), bf16[32,6,4096]{2,1,0:T(8,128)(2,1)}, u32[]{:S(2)}, u32[]{:S(2)}) %all-to-all-start) | async-done | bytes 1572896 | tf_op jit(solution)/shard_map/all_to_all | solution.py:86
  213.1 2.5 reshape.77
  215.6 0.0 all-gather.4.cloned.1.call-done
  215.6 2.4 fusion.13
  218.1 0.0 all-gather.6.cloned.1.call-done
  218.1 2.4 fusion.14
  220.6 0.0 all-gather.8.cloned.1.call-done
  220.6 3.4 convolution_convert_fusion.1
  224.0 3.7 reshape.85
  227.7 2.4 fusion.15
  230.1 0.6 fusion.1
  230.7 1.0 copy-done.4
  231.7 0.6 fusion
  232.3 1.6 reshape.89
  233.9 0.0 all-reduce.3.cloned.1.call-update
  234.0 39.4 %all-reduce.3.cloned.1.call-done = (bf16[32,6,4096]{2,1,0:T(8,128)(2,1)}, bf16[32,6,4096]{2,1,0:T(8,128)(2,1)}) async-done(((bf16[32,6,4096]{2,1,0:T(8,128)(2,1)}, bf16[32,6,4096]{2,1,0:T(8,128)(2,1)}), (bf16[32,6,4096]{2,1,0:T(8,128)(2,1)}, bf16[32,6,4096]{2,1,0:T(8,128)(2,1)})) %all-reduce.3.cloned.1.call-update) | async-done | bytes 3145744 | tf_op jit(solution)/shard_map/psum | solution.py:93
  273.4 57.0 %all_to_all.37 = bf16[32,6,4096]{2,1,0:T(8,128)(2,1)} all-to-all(bf16[32,6,4096]{2,1,0:T(8,128)(2,1)} %get-tuple-element.3), channel_id=1, replica_groups=mesh['dp'=4,'expert'=32,'tensor'=2] {'expert'}, dimensions={0} | all-to-all | bytes 3145728 | tf_op jit(solution)/shard_map/all_to_all | solution.py:99
  330.4 8.1 %all-to-all-start.6 = ((bf16[32,6,4096]{2,1,0:T(8,128)(2,1)}), bf16[32,6,4096]{2,1,0:T(8,128)(2,1)S(1)}, u32[]{:S(2)}, u32[]{:S(2)}) async-start(bf16[32,6,4096]{2,1,0:T(8,128)(2,1)} %get-tuple-element.4), calls=%async_computation.6 | async-start | bytes 4194304 | tf_op jit(solution)/shard_map/all_to_all | solution.py:100
  338.6 3.7 reshape.86
  342.2 2.9 convolution_convert_fusion.4
  345.1 42.2 %all-to-all-done.6 = bf16[32,6,4096]{2,1,0:T(8,128)(2,1)S(1)} async-done(((bf16[32,6,4096]{2,1,0:T(8,128)(2,1)}), bf16[32,6,4096]{2,1,0:T(8,128)(2,1)S(1)}, u32[]{:S(2)}, u32[]{:S(2)}) %all-to-all-start.6) | async-done | bytes 1572896 | tf_op jit(solution)/shard_map/all_to_all | solution.py:100
  387.3 1.5 reshape.90
  388.7 2.9 convolution_convert_fusion.3
  (23 shorter events, 0.1 us)
Async XLA Ops:
  7.2 78.3 %copy-start = (bf16[128,4096]{1,0:T(8,128)(2,1)S(1)}, bf16[128,4096]{1,0:T(8,128)(2,1)}, u32[]{:S(2)}) copy-start(bf16[128,4096]{1,0:T(8,128)(2,1)} %param.10) | copy-start | bytes 3145732
  7.2 6.0 %copy-start.1 = (bf16[231,1024]{1,0:T(8,128)(2,1)S(1)}, bf16[231,1024]{1,0:T(8,128)(2,1)}, u32[]{:S(2)}) copy-start(bf16[231,1024]{1,0:T(8,128)(2,1)} %param.15) | copy-start | bytes 1419268
  7.2 208.4 %all-gather.4.cloned.1.call-start = ((), (), s32[]{:S(2)}) async-start(), calls=%async_computation.7 | async-start | bytes 2621440 | tf_op jit(solution)/shard_map/all_gather | solution.py:60
  13.1 1.2 copy-start.2
  14.3 1.2 copy-start.3
  19.9 2.5 copy-start.8
  54.3 30.7 %copy-start.9 = (s32[128,1]{0,1:T(1,128)S(1)}, s32[128,1]{0,1:T(1,128)}, u32[]{:S(2)}) copy-start(s32[128,1]{0,1:T(1,128)} %param.11) | copy-start | bytes 1540
  78.7 23.6 %all-to-all-start.3 = ((bf16[64,4,1024]{2,1,0:T(4,128)(2,1)}), bf16[64,4,1024]{2,1,0:T(4,128)(2,1)S(1)}, u32[]{:S(2)}, u32[]{:S(2)}) async-start(bf16[64,4,1024]{2,1,0:T(4,128)(2,1)} %get-tuple-element.7), calls=%async_computation.3 | async-start | bytes 1048576 | tf_op jit(solution)/shard_map/all_to_all | solution.py:54
  102.3 0.8 copy-start.7
  103.1 54.2 %all-to-all-start.5 = ((bf16[32,6,4096]{2,1,0:T(8,128)(2,1)}), bf16[32,6,4096]{2,1,0:T(8,128)(2,1)S(1)}, u32[]{:S(2)}, u32[]{:S(2)}) async-start(bf16[32,6,4096]{2,1,0:T(8,128)(2,1)} %reshape.87), calls=%async_computation.5 | async-start | bytes 4194304 | tf_op jit(solution)/shard_map/all_to_all | solution.py:87
  108.3 109.8 %all-gather.6.cloned.1.call-start = ((), (), s32[]{:S(2)}) async-start(), calls=%async_computation.8 | async-start | bytes 2621440 | tf_op jit(solution)/shard_map/all_gather | solution.py:61
  157.3 55.8 %all-to-all-start = ((bf16[32,6,4096]{2,1,0:T(8,128)(2,1)}), bf16[32,6,4096]{2,1,0:T(8,128)(2,1)}, u32[]{:S(2)}, u32[]{:S(2)}) async-start(bf16[32,6,4096]{2,1,0:T(8,128)(2,1)} %reshape.76), calls=%async_computation | async-start | bytes 4194304 | tf_op jit(solution)/shard_map/all_to_all | solution.py:86
  164.4 56.2 %all-gather.8.cloned.1.call-start = ((), (), s32[]{:S(2)}) async-start(), calls=%async_computation.9 | async-start | bytes 2621440 | tf_op jit(solution)/shard_map/all_gather | solution.py:62
  166.4 107.0 %all-reduce.3.cloned.1.call-start = ((), (), s32[]{:S(2)}) async-start(), calls=%async_computation.10 | async-start | bytes 8388608 | tf_op jit(solution)/shard_map/psum | solution.py:93
  224.0 3.7 copy-start.5
  227.7 2.4 copy-start.6
  230.1 1.6 copy-start.4
  330.4 56.9 %all-to-all-start.6 = ((bf16[32,6,4096]{2,1,0:T(8,128)(2,1)}), bf16[32,6,4096]{2,1,0:T(8,128)(2,1)S(1)}, u32[]{:S(2)}, u32[]{:S(2)}) async-start(bf16[32,6,4096]{2,1,0:T(8,128)(2,1)} %get-tuple-element.4), calls=%async_computation.6 | async-start | bytes 4194304 | tf_op jit(solution)/shard_map/all_to_all | solution.py:100
Sparse Core Ops, SparseCore 0:
  55.4 30.2 all-gather.3
  110.9 34.8 all-gather.5
  167.6 35.0 all-gather.7
  234.1 39.2 all-reduce.2
where the time goes:
time: 400 us; the launch traced here: 398 us
  waiting for transfers between devices  182 us (46%)
  blocking collectives  111 us (28%)
  local copies, waits for them, and re-layouts  39.2 us (10%)
  starting transfers between devices  27 us (7%)
  matrix products  21.2 us (5%)
  between operations  14 us (4%)
  other arithmetic  4.47 us (1%)
    all_to_all x1, blocking collectives, per_device(): lax.all_to_all(out_back, 'expert', split_axis=0, concat_axis=0, tiled=True)  57 us
    all_to_all x1, waiting for transfers between devices, per_device(): lax.all_to_all(sent_tokens, 'expert', split_axis=0, concat_axis=0, tiled=...  45 us
    all_to_all x1, waiting for transfers between devices, per_device(): lax.all_to_all(grad_back, 'expert', split_axis=0, concat_axis=0, tiled=True)  42.2 us
    all_to_all x1, waiting for transfers between devices, per_device(): lax.all_to_all(sent_grads, 'expert', split_axis=0, concat_axis=0, tiled=T...  40.4 us
    psum x1, waiting for transfers between devices, per_device(): lax.psum(out_part.astype(jnp.bfloat16), 'tensor').astype(jnp.float32)  39.4 us
    all_to_all x1, blocking collectives, per_device(): lax.all_to_all(sent_gate, ('expert', 'tensor'), split_axis=0, concat_axis...  30 us
    all_to_all x1, blocking collectives, per_device(): lax.all_to_all(sent_up, ('expert', 'tensor'), split_axis=0, concat_axis=0...  23.5 us
    all_to_all x1, waiting for transfers between devices, per_device(): lax.all_to_all(sent_down, ('expert', 'tensor'), split_axis=0, concat_axis...  14.6 us
  transfers between devices with their start and end apart: 8, of which 5 were waited for; matrix products, arithmetic and copies ran while one was open for 7% of the time, Pallas kernels for 0%

commit v1 on v0

v1 whole, which is shorter than its diff:
```python
import functools

import jax
import jax.numpy as jnp
from jax import lax
from jax.experimental import pallas as pl
from jax.experimental.pallas import tpu as pltpu
from jax.sharding import PartitionSpec as P

NX, NZ = 4, 8
NE = NX * NZ
NDP = 4
CAP = 6
TILES = 3
CHUNKS = 2
PER = NE // CHUNKS
COLS = 1024
STEP = 512
LAG = 4
MESH = pl.DeviceIdType.MESH
BF = jnp.bfloat16
F32 = jnp.float32


def iota(shape, dim):
    return lax.broadcasted_iota(jnp.int32, shape, dim)


def onehot(mask):
    return jnp.where(mask, 1.0, 0.0).astype(BF)


def dot(a, b):
    return jnp.dot(a, b, preferred_element_type=F32)


def dot_t(a, b):
    return lax.dot_general(a, b, (((1,), (1,)), ((), ())), preferred_element_type=F32)


def displacement(i):
    j, k = i // NZ, lax.rem(i, NZ)
    dx = lax.rem(j, 2) * 2 + j // 2
    odd, half = lax.rem(k, 2), (k + 1) // 2
    dz = lax.rem(odd * half + (1 - odd) * (NZ - half), NZ)
    return dx, dz


def kernel(
    tok_ref,
    cot_ref,
    routes_ref,
    cluster_ref,
    wg_ref,
    wu_ref,
    wd_ref,
    out_ref,
    grad_ref,
    sel,
    ws,
    wr,
    ts,
    tr,
    xd,
    pre,
    ps,
    pr,
    own,
    ob,
    rs,
    hr,
    perm_in,
    perm_out,
    local_sem,
    w_send,
    w_recv,
    y_send,
    y_recv,
    t_send,
    t_recv,
    tf_send,
    tf_recv,
    p_send,
    p_recv,
    r_send,
    r_recv,
    rf_send,
    rf_recv,
):
    dp = lax.axis_index("dp")
    me = lax.axis_index("expert")
    core = lax.axis_index("tensor")
    mx, mz = me // NZ, lax.rem(me, NZ)
    shard = me * 2 + core
    rows_dev = wg_ref.shape[0]
    n_tok = tok_ref.shape[0]
    partner = (dp, me, 1 - core)

    def ahead(i):
        dx, dz = displacement(i)
        return lax.rem(mx + dx, NX) * NZ + lax.rem(mz + dz, NZ)

    def behind(i):
        dx, dz = displacement(i)
        return lax.rem(mx + NX - dx, NX) * NZ + lax.rem(mz + NZ - dz, NZ)

    def plane(step):
        return lax.rem(dp + NDP + step, NDP)

    def loop(lower, upper, body):
        def run(i, carry):
            body(i)
            return carry

        lax.fori_loop(lower, upper, run, 0)

    barrier = pltpu.get_barrier_semaphore()

    def greet(i):
        pl.semaphore_signal(barrier, 1, device_id=(dp, ahead(i), core), device_id_type=MESH)

    loop(1, NE, greet)
    pl.semaphore_signal(barrier, 1, device_id=(plane(1), me, core), device_id_type=MESH)
    pl.semaphore_signal(barrier, 1, device_id=(plane(-1), me, core), device_id_type=MESH)
    pl.semaphore_signal(barrier, 1, device_id=partner, device_id_type=MESH)

    half_slots = cluster_ref.shape[1] // 2
    sub = iota((8, 1), 0)
    slot = (sub // 4) * half_slots + shard * 4 + lax.rem(sub, 4)
    lanes = iota((8, cluster_ref.shape[1]), 1)
    neuron = iota((8, rows_dev), 1) + shard * rows_dev
    for e in range(NE):
        line = jnp.broadcast_to(cluster_ref[e : e + 1, :], lanes.shape)
        pick = jnp.sum(jnp.where(lanes == slot, line, 0), axis=1, keepdims=True)
        sel[e * 8 : e * 8 + 8, :] = jnp.where(neuron == pick, 1.0, 0.0)
    chosen = sel[...].astype(BF)
    for a, weight in enumerate((wg_ref, wu_ref, wd_ref)):
        for j in range(COLS // STEP):
            cols = slice(j * STEP, (j + 1) * STEP)
            ws.at[a].reshape(NE * 8, COLS)[:, cols] = dot(chosen, weight[:, cols]).astype(BF)

    pl.semaphore_wait(barrier, NE - 1 + 3)

    def weight_copy(i):
        return pltpu.make_async_remote_copy(
            src_ref=ws.at[:, ahead(i)],
            dst_ref=wr.at[dp, :, i],
            send_sem=w_send.at[i],
            recv_sem=w_recv.at[i],
            device_id=(dp, ahead(i), core),
            device_id_type=MESH,
        )

    own_weights = pltpu.make_async_copy(ws.at[:, me], wr.at[dp, :, 0], local_sem.at[0])
    own_weights.start()
    loop(1, NE, lambda i: weight_copy(i).start())

    square = (n_tok, n_tok)
    by_lane = jnp.broadcast_to(routes_ref[...], square)
    eye = iota(square, 0) == iota(square, 1)
    route_col = jnp.sum(jnp.where(eye, by_lane, 0), axis=1, keepdims=True)
    same = by_lane == route_col
    place_row = jnp.sum(
        jnp.where(same & (iota(square, 0) < iota(square, 1)), 1, 0), axis=0, keepdims=True
    )
    place_col = jnp.sum(
        jnp.where(same & (iota(square, 1) < iota(square, 0)), 1, 0), axis=1, keepdims=True
    )
    route_row = routes_ref[...]

    tall = (NE * 8, n_tok)
    row = iota(tall, 0)
    row_expert, row_sub = row // 8, lax.rem(row, 8)
    mine = row_expert == route_row
    for t in range(TILES):
        lhs = [onehot(mine & (place_row == row_sub + 8 * t - CAP * (t + j))) for j in range(2)]
        for c in range(COLS // STEP):
            total = None
            for j in range(2):
                block, source = (t + j) // 2, (tok_ref, cot_ref)[(t + j) % 2]
                first = pl.multiple_of(core * 2 * COLS + block * COLS + c * STEP, STEP)
                term = dot(lhs[j], source[:, pl.ds(first, STEP)])
                total = term if total is None else total + term
            ts.at[t].reshape(NE * 8, COLS)[:, c * STEP : (c + 1) * STEP] = total.astype(BF)

    def token_copy(i):
        return pltpu.make_async_remote_copy(
            src_ref=ts.at[:, ahead(i)],
            dst_ref=tr.at[core, i // PER, :, lax.rem(i, PER)],
            send_sem=t_send.at[i],
            recv_sem=t_recv.at[i],
            device_id=(dp, ahead(i), core),
            device_id_type=MESH,
        )

    own_tokens = pltpu.make_async_copy(ts.at[:, me], tr.at[core, 0, :, 0], local_sem.at[1])
    own_tokens.start()
    loop(1, NE, lambda i: token_copy(i).start())

    wide = (2 * CAP * PER, 2 * 8 * PER)
    r, q = iota(wide, 0), iota(wide, 1)
    a = jnp.where(r >= CAP * PER, 1, 0)
    t = jnp.where(q >= 8 * PER, 1, 0)
    r = r - a * (CAP * PER)
    q = q - t * (8 * PER)
    for h in range(2):
        p = lax.rem(q, 8) + 8 * (t + h) - CAP * (2 * h + a)
        perm_in[h] = onehot((p >= 0) & (p < CAP) & (r == CAP * (q // 8) + p))
    wide = (8 * PER, 2 * CAP * PER)
    r, q = iota(wide, 0), iota(wide, 1)
    j = jnp.where(q >= CAP * PER, 1, 0)
    q = q - j * (CAP * PER)
    for t in range(TILES):
        p = 2 * t + lax.rem(r, 8) - CAP * j
        perm_out[t] = onehot((p >= 0) & (p < CAP) & (q == CAP * (r // 8) + p))

    def plane_copy(i, which, step, slot_sem):
        return pltpu.make_async_remote_copy(
            src_ref=wr.at[which, :, i],
            dst_ref=wr.at[which, :, i],
            send_sem=y_send.at[slot_sem, i],
            recv_sem=y_recv.at[slot_sem, i],
            device_id=(plane(step), me, core),
            device_id_type=MESH,
        )

    def relay_copy(i):
        sign = 1 - 2 * lax.rem(i, 2)
        return plane_copy(i, plane(-sign), sign, 2)

    def spread(i):
        plane_copy(i, dp, 1, 0).start()
        plane_copy(i, dp, -1, 1).start()

    def relay(i):
        plane_copy(i, plane(-1), 1, 0).wait_recv()
        plane_copy(i, plane(1), -1, 1).wait_recv()
        relay_copy(i).start()

    own_weights.wait()
    spread(0)

    def weight_step(i):
        weight_copy(i).wait_recv()
        spread(i)

        @pl.when(i >= LAG)
        def _():
            relay(i - LAG)

    loop(1, NE, weight_step)
    loop(NE - LAG, NE, relay)

    def token_forward(i):
        return pltpu.make_async_remote_copy(
            src_ref=tr.at[core, i // PER, :, lax.rem(i, PER)],
            dst_ref=tr.at[core, i // PER, :, lax.rem(i, PER)],
            send_sem=tf_send.at[i],
            recv_sem=tf_recv.at[i],
            device_id=partner,
            device_id_type=MESH,
        )

    def token_step(i):
        token_copy(i).wait_recv()
        token_forward(i).start()

    own_tokens.wait()
    token_forward(0).start()
    loop(1, PER, token_step)
    loop(0, NE, lambda i: relay_copy(i).wait_recv())

    def return_copy(i):
        return pltpu.make_async_remote_copy(
            src_ref=rs.at[i // PER, :, lax.rem(i, PER)],
            dst_ref=hr.at[core, :, me],
            send_sem=r_send.at[i],
            recv_sem=r_recv.at[i],
            device_id=(dp, behind(i), core),
            device_id_type=MESH,
        )

    own_result = pltpu.make_async_copy(rs.at[0, :, 0], hr.at[core, :, me], local_sem.at[2])
    rows = CAP * PER
    for n in range(CHUNKS):
        if n:
            loop(n * PER, (n + 1) * PER, token_step)
        loop(n * PER, (n + 1) * PER, lambda i: token_forward(i).wait_recv())

        def unpack(b):
            half, h = b // 2, lax.rem(b, 2)
            source = tr.at[half, n, pl.ds(h, 2)].reshape(2 * 8 * PER, COLS)
            for c in range(COLS // STEP):
                cols = slice(c * STEP, (c + 1) * STEP)
                xd[b, :, cols] = dot(perm_in[h], source[:, cols]).astype(BF)

        loop(0, 4, unpack)
        pre[...] = jnp.zeros_like(pre)

        def project(b):
            gate_up = wr.at[b, pl.ds(0, 2)].reshape(2 * NE * 8, COLS)
            down = wr.at[b, 2].reshape(NE * 8, COLS)
            pre[:, : 2 * NE * 8] += dot_t(xd[b, :rows], gate_up[...])
            pre[:, 2 * NE * 8 :] += dot_t(xd[b, rows:], down[...])

        loop(0, 4, project)
        width = NE * 8
        gate, up, back = pre[:, :width], pre[:, width : 2 * width], pre[:, 2 * width :]
        s = jax.nn.sigmoid(gate)
        hidden = (gate * s * up).astype(BF)
        grad_gate = (back * up * s * (1.0 + gate * (1.0 - s))).astype(BF)
        grad_up = (back * gate * s).astype(BF)
        grads = jnp.concatenate([grad_gate, grad_up], axis=1)

        def part(b, put):
            gate_up = wr.at[b, pl.ds(0, 2)].reshape(2 * NE * 8, COLS)
            down = wr.at[b, 2].reshape(NE * 8, COLS)
            for c in range(COLS // STEP):
                cols = slice(c * STEP, (c + 1) * STEP)
                put(slice(0, rows), cols, dot(hidden, down[:, cols]))
                put(slice(rows, 2 * rows), cols, dot(grads, gate_up[:, cols]))

        def part_copy(h):
            return pltpu.make_async_remote_copy(
                src_ref=ps.at[n, h],
                dst_ref=pr.at[n, h],
                send_sem=p_send.at[n, h],
                recv_sem=p_recv.at[n, h],
                device_id=partner,
                device_id_type=MESH,
            )

        for h in range(2):

            def put_sent(at, cols, value):
                ps[n, h, at, cols] = value.astype(BF)

            part((1 - core) * 2 + h, put_sent)
            part_copy(h).start()
        for h in range(2):

            def put_own(at, cols, value):
                own[h, at, cols] = value.astype(BF)

            part(core * 2 + h, put_own)
        for h in range(2):
            part_copy(h).wait_recv()
            ob[h * 2 * rows : (h + 1) * 2 * rows, :] = (
                own[h].astype(F32) + pr[n, h].astype(F32)
            ).astype(BF)
        for t in range(TILES):
            for c in range(COLS // STEP):
                cols = slice(c * STEP, (c + 1) * STEP)
                moved = dot(perm_out[t], ob[t * rows : (t + 2) * rows, cols])
                rs.at[n, t].reshape(8 * PER, COLS)[:, cols] = moved.astype(BF)
        if n == 0:
            own_result.start()
            loop(1, PER, lambda i: return_copy(i).start())
        else:
            loop(n * PER, (n + 1) * PER, lambda i: return_copy(i).start())

    def result_forward(i):
        at = ahead(i)
        return pltpu.make_async_remote_copy(
            src_ref=hr.at[core, :, at],
            dst_ref=hr.at[core, :, at],
            send_sem=rf_send.at[i],
            recv_sem=rf_recv.at[i],
            device_id=partner,
            device_id_type=MESH,
        )

    def result_step(i):
        return_copy(i).wait_recv()
        result_forward(i).start()

    own_result.wait()
    result_forward(0).start()
    loop(1, NE, result_step)
    loop(0, NE, lambda i: result_forward(i).wait_recv())

    long = (n_tok, 2 * NE * 8)
    q = iota(long, 1)
    j = jnp.where(q >= NE * 8, 1, 0)
    q = q - j * (NE * 8)
    here = route_col == q // 8
    for h in range(2):
        table = jnp.concatenate(
            [
                onehot(here & (place_col == lax.rem(q, 8) + 8 * (h + j) - CAP * (2 * h + b)))
                for b in range(2)
            ],
            axis=0,
        )
        for half in range(2):
            source = hr.at[half, pl.ds(h, 2)].reshape(2 * NE * 8, COLS)
            for c in range(COLS // STEP):
                value = dot(table, source[:, c * STEP : (c + 1) * STEP]).astype(BF)
                first = (2 * half + h) * COLS + c * STEP
                out_ref[:, first : first + STEP] = value[:n_tok]
                grad_ref[:, first : first + STEP] = value[n_tok:]

    def drain(i):
        weight_copy(i).wait_send()
        token_copy(i).wait_send()
        return_copy(i).wait_send()

    loop(1, NE, drain)

    def drain_near(i):
        plane_copy(i, dp, 1, 0).wait_send()
        plane_copy(i, dp, -1, 1).wait_send()
        relay_copy(i).wait_send()
        token_forward(i).wait_send()
        result_forward(i).wait_send()

    loop(0, NE, drain_near)
    for n in range(CHUNKS):
        for h in range(2):
            pltpu.make_async_remote_copy(
                src_ref=ps.at[n, h],
                dst_ref=pr.at[n, h],
                send_sem=p_send.at[n, h],
                recv_sem=p_recv.at[n, h],
                device_id=partner,
                device_id_type=MESH,
            ).wait_send()


def per_device(tokens, cotangent, routes, cluster, w_gate, w_up, w_down):
    n_tok, width = tokens.shape
    rows_dev = w_gate.shape[0]
    dma = pltpu.SemaphoreType.DMA
    rows = CAP * PER
    vmem = pl.BlockSpec(memory_space=pltpu.VMEM)
    shape = jax.ShapeDtypeStruct((n_tok, width), BF)
    return pl.pallas_call(
        kernel,
        out_shape=(shape, shape),
        in_specs=[vmem] * 7,
        out_specs=(vmem, vmem),
        scratch_shapes=[
            pltpu.VMEM((NE * 8, rows_dev), F32),
            pltpu.VMEM((3, NE, 8, COLS), BF),
            pltpu.VMEM((NDP, 3, NE, 8, COLS), BF),
            pltpu.VMEM((TILES, NE, 8, COLS), BF),
            pltpu.VMEM((2, CHUNKS, TILES, PER, 8, COLS), BF),
            pltpu.VMEM((4, 2 * rows, COLS), BF),
            pltpu.VMEM((rows, 3 * NE * 8), F32),
            pltpu.VMEM((CHUNKS, 2, 2 * rows, COLS), BF),
            pltpu.VMEM((CHUNKS, 2, 2 * rows, COLS), BF),
            pltpu.VMEM((2, 2 * rows, COLS), BF),
            pltpu.VMEM((4 * rows, COLS), BF),
            pltpu.VMEM((CHUNKS, TILES, PER, 8, COLS), BF),
            pltpu.VMEM((2, TILES, NE, 8, COLS), BF),
            pltpu.VMEM((2, 2 * rows, 2 * 8 * PER), BF),
            pltpu.VMEM((TILES, 8 * PER, 2 * rows), BF),
            dma((3,)),
            dma((NE,)),
            dma((NE,)),
            dma((3, NE)),
            dma((3, NE)),
            dma((NE,)),
            dma((NE,)),
            dma((NE,)),
            dma((NE,)),
            dma((CHUNKS, 2)),
            dma((CHUNKS, 2)),
            dma((NE,)),
            dma((NE,)),
            dma((NE,)),
            dma((NE,)),
        ],
        compiler_params=pltpu.CompilerParams(
            collective_id=0, has_side_effects=True, vmem_limit_bytes=60 << 20
        ),
    )(tokens, cotangent, routes.reshape(1, n_tok), cluster, w_gate, w_up, w_down)


def solution(mesh):
    in_specs = (
        P(("dp", "expert"), None),
        P(("dp", "expert"), None),
        P(("dp", "expert"), None),
        P(),
        P(("expert", "tensor"), "dp"),
        P(("expert", "tensor"), "dp"),
        P(("expert", "tensor"), "dp"),
    )
    out_specs = (P(("dp", "expert"), None), P(("dp", "expert"), None))
    return jax.shard_map(
        per_device, mesh=mesh, in_specs=in_specs, out_specs=out_specs, check_vma=False
    )
```

time: 400 us -> 131 us (0.33)
  waiting for transfers between devices: 182 us -> 0 us
  Pallas kernels: 0 us -> 127 us
  blocking collectives: 111 us -> 0 us
  local copies, waits for them, and re-layouts: 39.2 us -> 3.35 us
  starting transfers between devices: 27 us -> 0 us
  matrix products: 21.2 us -> 0 us
  between operations: 14 us -> 0.65 us
  other arithmetic: 4.47 us -> 0 us
    all_to_all x4 -> x0, waiting for transfers between devices: 142 us -> none  [the longest x1 45 us: per_device(): lax.all_to_all(sent_tokens, 'expert', split_axis=0, concat_axis=0, tiled=...]
    pallas_call x0 -> x1, Pallas kernels: none -> 127 us  [per_device(): pl.pallas_call(kernel, out_shape=(shape, shape), in_specs=[vmem] * 7, out...]
    all_to_all x3 -> x0, blocking collectives: 111 us -> none  [the longest x1 57 us: per_device(): lax.all_to_all(out_back, 'expert', split_axis=0, concat_axis=0, tiled=True)]
    psum x1 -> x0, waiting for transfers between devices: 39.4 us -> none  [per_device(): lax.psum(out_part.astype(jnp.bfloat16), 'tensor').astype(jnp.float32)]
    reshape x15 -> x0, local copies, waits for them, and re-layouts: 31.7 us -> none  [the longest x1 4.46 us: per_device(): picks = cluster.reshape(shards, shards, per_shard)]
    all_to_all x4 -> x0, starting transfers between devices: 26.7 us -> none  [the longest x1 8.12 us: per_device(): lax.all_to_all(grad_back, 'expert', split_axis=0, concat_axis=0, tiled=True)]
    dot_general x10 -> x0, matrix products: 21.2 us -> none  [the longest x2 5.73 us: to_tokens(): lax.dot_general(dispatch_table, returned, contract, preferred_element_typ...]
    gather x3 -> x0, local copies, waits for them, and re-layouts: 4.3 us -> none  [select_rows(): jnp.take(weight, row_index, axis=0).reshape(shards, per_shard, width_part)]
  transfers between devices with their start and end apart: 8 -> 0, of which waited for: 5 -> 0; matrix products, arithmetic and copies ran while one was open for 7% -> 0% of each run, Pallas kernels for 0% -> 0%
where the time goes in v1:
time: 131 us
  Pallas kernels  127 us (97%)
  local copies, waits for them, and re-layouts  3.35 us (3%)
    pallas_call x1, Pallas kernels, per_device(): pl.pallas_call(kernel, out_shape=(shape, shape), in_specs=[vmem] * 7, out...  127 us
    unnamed x4, local copies, waits for them, and re-layouts  3.35 us

profile of v1, /device:TPU:1, one launch (start us, length us, event | category | flops | bytes accessed | tf_op | source)
XLA Modules:
  0.0 130.7 jit_solution(14636996017187714614)
XLA Ops:
  0.6 126.7 %shard_map.86 = (bf16[128,4096]{1,0:T(8,128)(2,1)}, bf16[128,4096]{1,0:T(8,128)(2,1)}) custom-call(bf16[128,4096]{1,0:T(8,128)(2,1)} %tok_ref.1, bf16[128,4096]{1,0:T(8,128)(2,1)} %cot_ref.1, s32[1,128]{1,0:T(1,128)} %bitcast.1, s32[32,512]{1,0:T(8,128)} %cluster_ref.1, bf16[231,1024]{1,0:T(8,128)(2,1)} %wg_ref.1, bf16[231,1024]{1,0:T(8,128)(2,1)} %wu_ref.1, ...), custom_call_target="tpu_custom_call" | custom-call | tf_op jit(solution)/shard_map/pallas_call | solution.py:437
  127.4 0.0 copy-start
  127.4 2.4 %copy.11 = bf16[128,4096]{1,0:T(8,128)(2,1)} copy(bf16[128,4096]{1,0:T(8,128)(2,1)} %get-tuple-element.4) | data formatting | bytes 2097152
  129.7 0.0 copy-done
  129.8 1.0 copy.12
Async XLA Ops:
  127.4 2.4 %copy-start = (bf16[128,4096]{1,0:T(8,128)(2,1)S(1)}, bf16[128,4096]{1,0:T(8,128)(2,1)}, u32[]{:S(2)}) copy-start(bf16[128,4096]{1,0:T(8,128)(2,1)} %get-tuple-element.5) | copy-start | bytes 3145732

commit v2 on v1

--- a/solution.py
+++ b/solution.py
@@ -16,8 +16,10 @@
 PER = NE // CHUNKS
 COLS = 1024
 STEP = 512
-LAG = 4
+GROUP = 4
+GROUPS = NE // GROUP
 MESH = pl.DeviceIdType.MESH
+VMEM_BYTES = 67_043_328 - (2 * TILES * NE * 8 * COLS + 2 * 256 * 512) * 2
 BF = jnp.bfloat16
 F32 = jnp.float32
 
@@ -38,24 +40,35 @@
     return lax.dot_general(a, b, (((1,), (1,)), ((), ())), preferred_element_type=F32)
 
 
-def displacement(i):
-    j, k = i // NZ, lax.rem(i, NZ)
-    dx = lax.rem(j, 2) * 2 + j // 2
+def along_z(k):
     odd, half = lax.rem(k, 2), (k + 1) // 2
-    dz = lax.rem(odd * half + (1 - odd) * (NZ - half), NZ)
-    return dx, dz
+    return lax.rem(odd * half + (1 - odd) * (NZ - half), NZ)
+
+
+def by_z(i):
+    return lax.rem(i, NX), along_z(i // NX)
+
+
+def by_x(i):
+    j = i // NZ
+    return lax.rem(j, 2) * 2 + j // 2, along_z(lax.rem(i, NZ))
 
 
 def kernel(
+    tok_hbm,
+    cot_hbm,
+    routes_hbm,
+    cluster_hbm,
+    wg_hbm,
+    wu_hbm,
+    wd_hbm,
+    hr,
+    table,
     tok_ref,
     cot_ref,
     routes_ref,
     cluster_ref,
-    wg_ref,
-    wu_ref,
-    wd_ref,
-    out_ref,
-    grad_ref,
+    w_ref,
     sel,
     ws,
     wr,
@@ -68,9 +81,9 @@
     own,
     ob,
     rs,
-    hr,
     perm_in,
     perm_out,
+    in_sem,
     local_sem,
     w_send,
     w_recv,
@@ -92,17 +105,15 @@
     core = lax.axis_index("tensor")
     mx, mz = me // NZ, lax.rem(me, NZ)
     shard = me * 2 + core
-    rows_dev = wg_ref.shape[0]
+    rows_dev = w_ref.shape[1]
     n_tok = tok_ref.shape[0]
     partner = (dp, me, 1 - core)
 
-    def ahead(i):
-        dx, dz = displacement(i)
-        return lax.rem(mx + dx, NX) * NZ + lax.rem(mz + dz, NZ)
-
-    def behind(i):
-        dx, dz = displacement(i)
-        return lax.rem(mx + NX - dx, NX) * NZ + lax.rem(mz + NZ - dz, NZ)
+    def ahead(step):
+        return lax.rem(mx + step[0], NX) * NZ + lax.rem(mz + step[1], NZ)
+
+    def behind(step):
+        return lax.rem(mx + NX - step[0], NX) * NZ + lax.rem(mz + NZ - step[1], NZ)
 
     def plane(step):
         return lax.rem(dp + NDP + step, NDP)
@@ -117,12 +128,30 @@
     barrier = pltpu.get_barrier_semaphore()
 
     def greet(i):
-        pl.semaphore_signal(barrier, 1, device_id=(dp, ahead(i), core), device_id_type=MESH)
+        pl.semaphore_signal(barrier, 1, device_id=(dp, ahead(by_z(NE - i)), core), device_id_type=MESH)
 
     loop(1, NE, greet)
     pl.semaphore_signal(barrier, 1, device_id=(plane(1), me, core), device_id_type=MESH)
     pl.semaphore_signal(barrier, 1, device_id=(plane(-1), me, core), device_id_type=MESH)
     pl.semaphore_signal(barrier, 1, device_id=partner, device_id_type=MESH)
+
+    pulls = [
+        pltpu.make_async_copy(source, target, in_sem.at[k])
+        for k, (source, target) in enumerate(
+            (
+                (cluster_hbm, cluster_ref),
+                (wg_hbm, w_ref.at[0]),
+                (wu_hbm, w_ref.at[1]),
+                (wd_hbm, w_ref.at[2]),
+                (routes_hbm, routes_ref),
+                (tok_hbm, tok_ref),
+                (cot_hbm, cot_ref),
+            )
+        )
+    ]
+    for pull in pulls:
+        pull.start()
+    pulls[0].wait()
 
     half_slots = cluster_ref.shape[1] // 2
     sub = iota((8, 1), 0)
@@ -134,26 +163,51 @@
         pick = jnp.sum(jnp.where(lanes == slot, line, 0), axis=1, keepdims=True)
         sel[e * 8 : e * 8 + 8, :] = jnp.where(neuron == pick, 1.0, 0.0)
     chosen = sel[...].astype(BF)
-    for a, weight in enumerate((wg_ref, wu_ref, wd_ref)):
+    for a in range(3):
+        pulls[1 + a].wait()
         for j in range(COLS // STEP):
             cols = slice(j * STEP, (j + 1) * STEP)
-            ws.at[a].reshape(NE * 8, COLS)[:, cols] = dot(chosen, weight[:, cols]).astype(BF)
+            ws.at[a].reshape(NE * 8, COLS)[:, cols] = dot(chosen, w_ref[a, :, cols]).astype(BF)
 
     pl.semaphore_wait(barrier, NE - 1 + 3)
 
     def weight_copy(i):
+        to = ahead(by_z(i))
         return pltpu.make_async_remote_copy(
-            src_ref=ws.at[:, ahead(i)],
+            src_ref=ws.at[:, to],
             dst_ref=wr.at[dp, :, i],
-            send_sem=w_send.at[i],
-            recv_sem=w_recv.at[i],
-            device_id=(dp, ahead(i), core),
+            send_sem=w_send.at[0],
+            recv_sem=w_recv.at[i // GROUP],
+            device_id=(dp, to, core),
             device_id_type=MESH,
         )
 
     own_weights = pltpu.make_async_copy(ws.at[:, me], wr.at[dp, :, 0], local_sem.at[0])
     own_weights.start()
     loop(1, NE, lambda i: weight_copy(i).start())
+
+    def landed(ref, sem):
+        pltpu.make_async_remote_copy(
+            src_ref=ref,
+            dst_ref=ref,
+            send_sem=local_sem.at[3],
+            recv_sem=sem,
+            device_id=partner,
+            device_id_type=MESH,
+        ).wait_recv()
+
+    def left(ref, sem):
+        pltpu.make_async_remote_copy(
+            src_ref=ref,
+            dst_ref=ref,
+            send_sem=sem,
+            recv_sem=local_sem.at[3],
+            device_id=partner,
+            device_id_type=MESH,
+        ).wait_send()
+
+    for pull in pulls[4:]:
+        pull.wait()
 
     square = (n_tok, n_tok)
     by_lane = jnp.broadcast_to(routes_ref[...], square)
@@ -184,18 +238,29 @@
             ts.at[t].reshape(NE * 8, COLS)[:, c * STEP : (c + 1) * STEP] = total.astype(BF)
 
     def token_copy(i):
+        to = ahead(by_x(i))
         return pltpu.make_async_remote_copy(
-            src_ref=ts.at[:, ahead(i)],
+            src_ref=ts.at[:, to],
             dst_ref=tr.at[core, i // PER, :, lax.rem(i, PER)],
-            send_sem=t_send.at[i],
-            recv_sem=t_recv.at[i],
-            device_id=(dp, ahead(i), core),
+            send_sem=t_send.at[0],
+            recv_sem=t_recv.at[i // GROUP],
+            device_id=(dp, to, core),
             device_id_type=MESH,
         )
 
     own_tokens = pltpu.make_async_copy(ts.at[:, me], tr.at[core, 0, :, 0], local_sem.at[1])
     own_tokens.start()
     loop(1, NE, lambda i: token_copy(i).start())
+
+    long = (n_tok, 2 * NE * 8)
+    q = iota(long, 1)
+    j = jnp.where(q >= NE * 8, 1, 0)
+    q = q - j * (NE * 8)
+    here = route_col == ahead(by_x(q // 8))
+    for h in range(2):
+        for b in range(2):
+            spot = place_col == lax.rem(q, 8) + 8 * (h + j) - CAP * (2 * h + b)
+            table[h, b * n_tok : (b + 1) * n_tok, :] = onehot(here & spot)
 
     wide = (2 * CAP * PER, 2 * 8 * PER)
     r, q = iota(wide, 0), iota(wide, 1)
@@ -214,78 +279,82 @@
         p = 2 * t + lax.rem(r, 8) - CAP * j
         perm_out[t] = onehot((p >= 0) & (p < CAP) & (q == CAP * (r // 8) + p))
 
-    def plane_copy(i, which, step, slot_sem):
+    def plane_copy(g, which, step, way):
+        group = wr.at[which, :, pl.ds(g * GROUP, GROUP)]
         return pltpu.make_async_remote_copy(
-            src_ref=wr.at[which, :, i],
-            dst_ref=wr.at[which, :, i],
-            send_sem=y_send.at[slot_sem, i],
-            recv_sem=y_recv.at[slot_sem, i],
+            src_ref=group,
+            dst_ref=group,
+            send_sem=y_send.at[0],
+            recv_sem=y_recv.at[way, g],
             device_id=(plane(step), me, core),
             device_id_type=MESH,
         )
 
-    def relay_copy(i):
-        sign = 1 - 2 * lax.rem(i, 2)
-        return plane_copy(i, plane(-sign), sign, 2)
-
-    def spread(i):
-        plane_copy(i, dp, 1, 0).start()
-        plane_copy(i, dp, -1, 1).start()
-
-    def relay(i):
-        plane_copy(i, plane(-1), 1, 0).wait_recv()
-        plane_copy(i, plane(1), -1, 1).wait_recv()
-        relay_copy(i).start()
+    def relay_copy(g):
+        sign = 1 - 2 * lax.rem(g, 2)
+        return plane_copy(g, plane(-sign), sign, 2)
+
+    def spread(g):
+        plane_copy(g, dp, 1, 0).start()
+        plane_copy(g, dp, -1, 1).start()
+
+    def relay(g):
+        plane_copy(g, plane(-1), 1, 0).wait_recv()
+        plane_copy(g, plane(1), -1, 1).wait_recv()
+        relay_copy(g).start()
 
     own_weights.wait()
+    landed(wr.at[dp, :, pl.ds(1, GROUP - 1)], w_recv.at[0])
     spread(0)
 
-    def weight_step(i):
-        weight_copy(i).wait_recv()
-        spread(i)
-
-        @pl.when(i >= LAG)
-        def _():
-            relay(i - LAG)
-
-    loop(1, NE, weight_step)
-    loop(NE - LAG, NE, relay)
-
-    def token_forward(i):
+    def weight_step(g):
+        landed(wr.at[dp, :, pl.ds(g * GROUP, GROUP)], w_recv.at[g])
+        spread(g)
+        relay(g - 1)
+
+    loop(1, GROUPS, weight_step)
+    relay(GROUPS - 1)
+
+    def token_group(g):
+        per = PER // GROUP
+        return tr.at[core, g // per, :, pl.ds(lax.rem(g, per) * GROUP, GROUP)]
+
+    def token_forward(g):
         return pltpu.make_async_remote_copy(
-            src_ref=tr.at[core, i // PER, :, lax.rem(i, PER)],
-            dst_ref=tr.at[core, i // PER, :, lax.rem(i, PER)],
-            send_sem=tf_send.at[i],
-            recv_sem=tf_recv.at[i],
+            src_ref=token_group(g),
+            dst_ref=token_group(g),
+            send_sem=tf_send.at[0],
+            recv_sem=tf_recv.at[g // (PER // GROUP)],
             device_id=partner,
             device_id_type=MESH,
         )
 
-    def token_step(i):
-        token_copy(i).wait_recv()
-        token_forward(i).start()
+    def token_step(g):
+        landed(token_group(g), t_recv.at[g])
+        token_forward(g).start()
 
     own_tokens.wait()
+    landed(tr.at[core, 0, :, pl.ds(1, GROUP - 1)], t_recv.at[0])
     token_forward(0).start()
-    loop(1, PER, token_step)
-    loop(0, NE, lambda i: relay_copy(i).wait_recv())
+    loop(1, PER // GROUP, token_step)
+    loop(0, GROUPS, lambda g: relay_copy(g).wait_recv())
 
     def return_copy(i):
         return pltpu.make_async_remote_copy(
             src_ref=rs.at[i // PER, :, lax.rem(i, PER)],
-            dst_ref=hr.at[core, :, me],
-            send_sem=r_send.at[i],
-            recv_sem=r_recv.at[i],
-            device_id=(dp, behind(i), core),
-            device_id_type=MESH,
-        )
-
-    own_result = pltpu.make_async_copy(rs.at[0, :, 0], hr.at[core, :, me], local_sem.at[2])
+            dst_ref=hr.at[core, :, i],
+            send_sem=r_send.at[0],
+            recv_sem=r_recv.at[i // GROUP],
+            device_id=(dp, behind(by_x(i)), core),
+            device_id_type=MESH,
+        )
+
+    own_result = pltpu.make_async_copy(rs.at[0, :, 0], hr.at[core, :, 0], local_sem.at[2])
     rows = CAP * PER
     for n in range(CHUNKS):
         if n:
-            loop(n * PER, (n + 1) * PER, token_step)
-        loop(n * PER, (n + 1) * PER, lambda i: token_forward(i).wait_recv())
+            loop(n * PER // GROUP, (n + 1) * PER // GROUP, token_step)
+        landed(tr.at[1 - core, n], tf_recv.at[n])
 
         def unpack(b):
             half, h = b // 2, lax.rem(b, 2)
@@ -359,72 +428,48 @@
         else:
             loop(n * PER, (n + 1) * PER, lambda i: return_copy(i).start())
 
-    def result_forward(i):
-        at = ahead(i)
+    def result_forward(g):
+        group = hr.at[core, :, pl.ds(g * GROUP, GROUP)]
         return pltpu.make_async_remote_copy(
-            src_ref=hr.at[core, :, at],
-            dst_ref=hr.at[core, :, at],
-            send_sem=rf_send.at[i],
-            recv_sem=rf_recv.at[i],
+            src_ref=group,
+            dst_ref=group,
+            send_sem=rf_send.at[0],
+            recv_sem=rf_recv.at[0],
             device_id=partner,
             device_id_type=MESH,
         )
 
-    def result_step(i):
-        return_copy(i).wait_recv()
-        result_forward(i).start()
+    def result_step(g):
+        landed(hr.at[core, :, pl.ds(g * GROUP, GROUP)], r_recv.at[g])
+        result_forward(g).start()
 
     own_result.wait()
+    landed(hr.at[core, :, pl.ds(1, GROUP - 1)], r_recv.at[0])
     result_forward(0).start()
-    loop(1, NE, result_step)
-    loop(0, NE, lambda i: result_forward(i).wait_recv())
-
-    long = (n_tok, 2 * NE * 8)
-    q = iota(long, 1)
-    j = jnp.where(q >= NE * 8, 1, 0)
-    q = q - j * (NE * 8)
-    here = route_col == q // 8
-    for h in range(2):
-        table = jnp.concatenate(
-            [
-                onehot(here & (place_col == lax.rem(q, 8) + 8 * (h + j) - CAP * (2 * h + b)))
-                for b in range(2)
-            ],
-            axis=0,
-        )
-        for half in range(2):
-            source = hr.at[half, pl.ds(h, 2)].reshape(2 * NE * 8, COLS)
-            for c in range(COLS // STEP):
-                value = dot(table, source[:, c * STEP : (c + 1) * STEP]).astype(BF)
-                first = (2 * half + h) * COLS + c * STEP
-                out_ref[:, first : first + STEP] = value[:n_tok]
-                grad_ref[:, first : first + STEP] = value[n_tok:]
-
-    def drain(i):
-        weight_copy(i).wait_send()
-        token_copy(i).wait_send()
-        return_copy(i).wait_send()
-
-    loop(1, NE, drain)
-
-    def drain_near(i):
-        plane_copy(i, dp, 1, 0).wait_send()
-        plane_copy(i, dp, -1, 1).wait_send()
-        relay_copy(i).wait_send()
-        token_forward(i).wait_send()
-        result_forward(i).wait_send()
-
-    loop(0, NE, drain_near)
+    loop(1, GROUPS, result_step)
+
+    left(ws.at[:, pl.ds(0, NE - 1)], w_send.at[0])
+    left(ts.at[:, pl.ds(0, NE - 1)], t_send.at[0])
+    left(hr.at[core, :, pl.ds(0, NE - 1)], r_send.at[0])
+    left(wr.at[pl.ds(0, 3)], y_send.at[0])
+    left(tr.at[core], tf_send.at[0])
     for n in range(CHUNKS):
         for h in range(2):
-            pltpu.make_async_remote_copy(
-                src_ref=ps.at[n, h],
-                dst_ref=pr.at[n, h],
-                send_sem=p_send.at[n, h],
-                recv_sem=p_recv.at[n, h],
-                device_id=partner,
-                device_id_type=MESH,
-            ).wait_send()
+            left(ps.at[n, h], p_send.at[n, h])
+    left(hr.at[core], rf_send.at[0])
+    landed(hr.at[1 - core], rf_recv.at[0])
+
+
+def finish(hr, table, out_ref, grad_ref):
+    b = pl.program_id(0)
+    half, h = b // 2, lax.rem(b, 2)
+    n_tok = out_ref.shape[0]
+    source = hr.at[half, pl.ds(h, 2)].reshape(2 * NE * 8, COLS)
+    for c in range(COLS // STEP):
+        cols = slice(c * STEP, (c + 1) * STEP)
+        value = dot(table[h], source[:, cols]).astype(BF)
+        out_ref[:, cols] = value[:n_tok]
+        grad_ref[:, cols] = value[n_tok:]
 
 
 def per_device(tokens, cotangent, routes, cluster, w_gate, w_up, w_down):
@@ -433,13 +478,20 @@
     dma = pltpu.SemaphoreType.DMA
     rows = CAP * PER
     vmem = pl.BlockSpec(memory_space=pltpu.VMEM)
-    shape = jax.ShapeDtypeStruct((n_tok, width), BF)
-    return pl.pallas_call(
+    results, table = pl.pallas_call(
         kernel,
-        out_shape=(shape, shape),
-        in_specs=[vmem] * 7,
+        out_shape=(
+            pltpu.VMEM((2, TILES, NE, 8, COLS), BF),
+            pltpu.VMEM((2, 2 * n_tok, 2 * NE * 8), BF),
+        ),
+        in_specs=[pl.BlockSpec(memory_space=pltpu.HBM)] * 7,
         out_specs=(vmem, vmem),
         scratch_shapes=[
+            pltpu.VMEM((n_tok, width), BF),
+            pltpu.VMEM((n_tok, width), BF),
+            pltpu.VMEM((1, n_tok), jnp.int32),
+            pltpu.VMEM(cluster.shape, jnp.int32),
+            pltpu.VMEM((3, rows_dev, w_gate.shape[1]), BF),
             pltpu.VMEM((NE * 8, rows_dev), F32),
             pltpu.VMEM((3, NE, 8, COLS), BF),
             pltpu.VMEM((NDP, 3, NE, 8, COLS), BF),
@@ -452,29 +504,39 @@
             pltpu.VMEM((2, 2 * rows, COLS), BF),
             pltpu.VMEM((4 * rows, COLS), BF),
             pltpu.VMEM((CHUNKS, TILES, PER, 8, COLS), BF),
-            pltpu.VMEM((2, TILES, NE, 8, COLS), BF),
             pltpu.VMEM((2, 2 * rows, 2 * 8 * PER), BF),
             pltpu.VMEM((TILES, 8 * PER, 2 * rows), BF),
-            dma((3,)),
-            dma((NE,)),
-            dma((NE,)),
-            dma((3, NE)),
-            dma((3, NE)),
-            dma((NE,)),
-            dma((NE,)),
-            dma((NE,)),
-            dma((NE,)),
+            dma((7,)),
+            dma((4,)),
+            dma((1,)),
+            dma((GROUPS,)),
+            dma((1,)),
+            dma((3, GROUPS)),
+            dma((1,)),
+            dma((GROUPS,)),
+            dma((1,)),
+            dma((CHUNKS,)),
             dma((CHUNKS, 2)),
             dma((CHUNKS, 2)),
-            dma((NE,)),
-            dma((NE,)),
-            dma((NE,)),
-            dma((NE,)),
+            dma((1,)),
+            dma((GROUPS,)),
+            dma((1,)),
+            dma((1,)),
         ],
         compiler_params=pltpu.CompilerParams(
-            collective_id=0, has_side_effects=True, vmem_limit_bytes=60 << 20
+            collective_id=0, has_side_effects=True, vmem_limit_bytes=VMEM_BYTES
         ),
     )(tokens, cotangent, routes.reshape(1, n_tok), cluster, w_gate, w_up, w_down)
+    column = pl.BlockSpec((n_tok, COLS), lambda b: (0, b))
+    shape = jax.ShapeDtypeStruct((n_tok, width), BF)
+    return pl.pallas_call(
+        finish,
+        grid=(width // COLS,),
+        out_shape=(shape, shape),
+        in_specs=[vmem, vmem],
+        out_specs=(column, column),
+        compiler_params=pltpu.CompilerParams(vmem_limit_bytes=16 << 20),
+    )(results, table)
 
 
 def solution(mesh):

time: 131 us -> 121 us (0.924)
  Pallas kernels: 127 us -> 120 us
  local copies, waits for them, and re-layouts: 3.35 us -> 0 us
    pallas_call x1 -> x2, Pallas kernels: 127 us -> 120 us  [the longest x1 117 us: per_device(): pl.pallas_call(kernel, out_shape=(pltpu.VMEM((2, TILES, NE, 8, COLS), BF)...]
    unnamed x4 -> x0, local copies, waits for them, and re-layouts: 3.35 us -> none
where the time goes in v2:
time: 121 us
  Pallas kernels  120 us (99%)
    pallas_call x1, Pallas kernels, per_device(): pl.pallas_call(kernel, out_shape=(pltpu.VMEM((2, TILES, NE, 8, COLS), BF)...  117 us
    pallas_call x1, Pallas kernels, per_device(): pl.pallas_call(finish, grid=(width // COLS,), out_shape=(shape, shape), i...  2.88 us

profile of v2, /device:TPU:1, one launch (start us, length us, event | category | flops | bytes accessed | tf_op | source)
XLA Modules:
  0.0 120.6 jit_solution(13349260772826468570)
XLA Ops:
  0.6 117.1 %shard_map.86 = (bf16[2,3,32,8,1024]{4,3,2,1,0:T(8,128)(2,1)S(1)}, bf16[2,256,512]{2,1,0:T(8,128)(2,1)S(1)}) custom-call(bf16[128,4096]{1,0:T(8,128)(2,1)} %tok_hbm.1, bf16[128,4096]{1,0:T(8,128)(2,1)} %cot_hbm.1, s32[1,128]{1,0:T(1,128)} %bitcast.1, s32[32,512]{1,0:T(8,128)} %cluster_hbm.1, bf16[231,1024]{1,0:T(8,128)(2,1)} %wg_hbm.1, ...), custom_call_target="tpu_custom_call" | custom-call | tf_op jit(solution)/shard_map/pallas_call | solution.py:481
  117.7 2.9 %shard_map.87 = (bf16[128,4096]{1,0:T(8,128)(2,1)}, bf16[128,4096]{1,0:T(8,128)(2,1)}) custom-call(bf16[2,3,32,8,1024]{4,3,2,1,0:T(8,128)(2,1)S(1)} %get-tuple-element.4.hr, bf16[2,256,512]{2,1,0:T(8,128)(2,1)S(1)} %get-tuple-element.5.table), custom_call_target="tpu_custom_call" | custom-call | tf_op jit(solution)/shard_map/pallas_call | solution.py:532

commit v3 on v2

--- a/solution.py
+++ b/solution.py
@@ -18,8 +18,11 @@
 STEP = 512
 GROUP = 4
 GROUPS = NE // GROUP
+LAST = NE - GROUP
+STEPS = [(dx, dz) for dz in (0, 1, 7, 2, 6, 3, 5, 4) for dx in range(NX)]
+HOME = STEPS.index((0, 0))
 MESH = pl.DeviceIdType.MESH
-VMEM_BYTES = 67_043_328 - (2 * TILES * NE * 8 * COLS + 2 * 256 * 512) * 2
+VMEM_BYTES = 67_043_328 - (2 * TILES * NE * 8 * COLS + 4 * 256 * 256 + 4 * 256 * COLS) * 2
 BF = jnp.bfloat16
 F32 = jnp.float32
 
@@ -43,10 +46,6 @@
 def along_z(k):
     odd, half = lax.rem(k, 2), (k + 1) // 2
     return lax.rem(odd * half + (1 - odd) * (NZ - half), NZ)
-
-
-def by_z(i):
-    return lax.rem(i, NX), along_z(i // NX)
 
 
 def by_x(i):
@@ -64,6 +63,7 @@
     wd_hbm,
     hr,
     table,
+    part_out,
     tok_ref,
     cot_ref,
     routes_ref,
@@ -125,16 +125,6 @@
 
         lax.fori_loop(lower, upper, run, 0)
 
-    barrier = pltpu.get_barrier_semaphore()
-
-    def greet(i):
-        pl.semaphore_signal(barrier, 1, device_id=(dp, ahead(by_z(NE - i)), core), device_id_type=MESH)
-
-    loop(1, NE, greet)
-    pl.semaphore_signal(barrier, 1, device_id=(plane(1), me, core), device_id_type=MESH)
-    pl.semaphore_signal(barrier, 1, device_id=(plane(-1), me, core), device_id_type=MESH)
-    pl.semaphore_signal(barrier, 1, device_id=partner, device_id_type=MESH)
-
     pulls = [
         pltpu.make_async_copy(source, target, in_sem.at[k])
         for k, (source, target) in enumerate(
@@ -149,42 +139,57 @@
             )
         )
     ]
-    for pull in pulls:
+    for pull in pulls[:4]:
         pull.start()
-    pulls[0].wait()
+
+    barrier = pltpu.get_barrier_semaphore()
+    for step in reversed(STEPS):
+        if step != (0, 0):
+            pl.semaphore_signal(barrier, 1, device_id=(dp, ahead(step), core), device_id_type=MESH)
+    pl.semaphore_signal(barrier, 1, device_id=(plane(1), me, core), device_id_type=MESH)
+    pl.semaphore_signal(barrier, 1, device_id=(plane(-1), me, core), device_id_type=MESH)
+    pl.semaphore_signal(barrier, 1, device_id=partner, device_id_type=MESH)
+    for pull in pulls[4:]:
+        pull.start()
+
+    def weight_copy(i):
+        return pltpu.make_async_remote_copy(
+            src_ref=ws.at[:, i],
+            dst_ref=wr.at[dp, :, i],
+            send_sem=w_send.at[0],
+            recv_sem=w_recv.at[i // GROUP],
+            device_id=(dp, ahead(STEPS[i]), core),
+            device_id_type=MESH,
+        )
 
     half_slots = cluster_ref.shape[1] // 2
     sub = iota((8, 1), 0)
     slot = (sub // 4) * half_slots + shard * 4 + lax.rem(sub, 4)
     lanes = iota((8, cluster_ref.shape[1]), 1)
     neuron = iota((8, rows_dev), 1) + shard * rows_dev
-    for e in range(NE):
-        line = jnp.broadcast_to(cluster_ref[e : e + 1, :], lanes.shape)
-        pick = jnp.sum(jnp.where(lanes == slot, line, 0), axis=1, keepdims=True)
-        sel[e * 8 : e * 8 + 8, :] = jnp.where(neuron == pick, 1.0, 0.0)
-    chosen = sel[...].astype(BF)
-    for a in range(3):
-        pulls[1 + a].wait()
-        for j in range(COLS // STEP):
-            cols = slice(j * STEP, (j + 1) * STEP)
-            ws.at[a].reshape(NE * 8, COLS)[:, cols] = dot(chosen, w_ref[a, :, cols]).astype(BF)
-
-    pl.semaphore_wait(barrier, NE - 1 + 3)
-
-    def weight_copy(i):
-        to = ahead(by_z(i))
-        return pltpu.make_async_remote_copy(
-            src_ref=ws.at[:, to],
-            dst_ref=wr.at[dp, :, i],
-            send_sem=w_send.at[0],
-            recv_sem=w_recv.at[i // GROUP],
-            device_id=(dp, to, core),
-            device_id_type=MESH,
-        )
-
-    own_weights = pltpu.make_async_copy(ws.at[:, me], wr.at[dp, :, 0], local_sem.at[0])
-    own_weights.start()
-    loop(1, NE, lambda i: weight_copy(i).start())
+    own_weights = pltpu.make_async_copy(ws.at[:, HOME], wr.at[dp, :, HOME], local_sem.at[0])
+    pulls[0].wait()
+    for g in range(GROUPS):
+        pieces = range(g * GROUP, (g + 1) * GROUP)
+        for i in pieces:
+            line = jnp.broadcast_to(cluster_ref[pl.ds(ahead(STEPS[i]), 1), :], lanes.shape)
+            pick = jnp.sum(jnp.where(lanes == slot, line, 0), axis=1, keepdims=True)
+            sel[i * 8 : i * 8 + 8, :] = jnp.where(neuron == pick, 1.0, 0.0)
+        chosen = sel[g * GROUP * 8 : (g + 1) * GROUP * 8, :].astype(BF)
+        for a in range(3):
+            if g == 0:
+                pulls[1 + a].wait()
+            picked = ws.at[a, g * GROUP : (g + 1) * GROUP].reshape(GROUP * 8, COLS)
+            picked[...] = dot(chosen, w_ref[a]).astype(BF)
+        if g == 1:
+            pl.semaphore_wait(barrier, NE - 1 + 3)
+        if g == 0:
+            continue
+        for i in range(g * GROUP if g > 1 else 0, (g + 1) * GROUP):
+            if i == HOME:
+                own_weights.start()
+            else:
+                weight_copy(i).start()
 
     def landed(ref, sem):
         pltpu.make_async_remote_copy(
@@ -252,15 +257,16 @@
     own_tokens.start()
     loop(1, NE, lambda i: token_copy(i).start())
 
-    long = (n_tok, 2 * NE * 8)
+    long = (n_tok, 2 * 8 * PER)
     q = iota(long, 1)
-    j = jnp.where(q >= NE * 8, 1, 0)
-    q = q - j * (NE * 8)
-    here = route_col == ahead(by_x(q // 8))
-    for h in range(2):
-        for b in range(2):
-            spot = place_col == lax.rem(q, 8) + 8 * (h + j) - CAP * (2 * h + b)
-            table[h, b * n_tok : (b + 1) * n_tok, :] = onehot(here & spot)
+    j = jnp.where(q >= 8 * PER, 1, 0)
+    q = q - j * (8 * PER)
+    for n in range(CHUNKS):
+        here = route_col == ahead(by_x(q // 8 + n * PER))
+        for h in range(2):
+            for b in range(2):
+                spot = place_col == lax.rem(q, 8) + 8 * (h + j) - CAP * (2 * h + b)
+                table[n, h, b * n_tok : (b + 1) * n_tok, :] = onehot(here & spot)
 
     wide = (2 * CAP * PER, 2 * 8 * PER)
     r, q = iota(wide, 0), iota(wide, 1)
@@ -303,16 +309,15 @@
         plane_copy(g, plane(1), -1, 1).wait_recv()
         relay_copy(g).start()
 
-    own_weights.wait()
-    landed(wr.at[dp, :, pl.ds(1, GROUP - 1)], w_recv.at[0])
-    spread(0)
-
-    def weight_step(g):
-        landed(wr.at[dp, :, pl.ds(g * GROUP, GROUP)], w_recv.at[g])
+    for g in range(GROUPS):
+        if g == HOME // GROUP:
+            own_weights.wait()
+            landed(wr.at[dp, :, pl.ds(g * GROUP + 1, GROUP - 1)], w_recv.at[g])
+        else:
+            landed(wr.at[dp, :, pl.ds(g * GROUP, GROUP)], w_recv.at[g])
         spread(g)
-        relay(g - 1)
-
-    loop(1, GROUPS, weight_step)
+        if g:
+            relay(g - 1)
     relay(GROUPS - 1)
 
     def token_group(g):
@@ -337,19 +342,18 @@
     landed(tr.at[core, 0, :, pl.ds(1, GROUP - 1)], t_recv.at[0])
     token_forward(0).start()
     loop(1, PER // GROUP, token_step)
-    loop(0, GROUPS, lambda g: relay_copy(g).wait_recv())
 
     def return_copy(i):
         return pltpu.make_async_remote_copy(
             src_ref=rs.at[i // PER, :, lax.rem(i, PER)],
-            dst_ref=hr.at[core, :, i],
+            dst_ref=hr.at[core, i // PER, :, lax.rem(i, PER)],
             send_sem=r_send.at[0],
-            recv_sem=r_recv.at[i // GROUP],
+            recv_sem=r_recv.at[i // GROUP + (i // LAST) * (i - LAST)],
             device_id=(dp, behind(by_x(i)), core),
             device_id_type=MESH,
         )
 
-    own_result = pltpu.make_async_copy(rs.at[0, :, 0], hr.at[core, :, 0], local_sem.at[2])
+    own_result = pltpu.make_async_copy(rs.at[0, :, 0], hr.at[core, 0, :, 0], local_sem.at[2])
     rows = CAP * PER
     for n in range(CHUNKS):
         if n:
@@ -372,7 +376,12 @@
             pre[:, : 2 * NE * 8] += dot_t(xd[b, :rows], gate_up[...])
             pre[:, 2 * NE * 8 :] += dot_t(xd[b, rows:], down[...])
 
-        loop(0, 4, project)
+        project(dp)
+        project(plane(1))
+        project(plane(-1))
+        if n == 0:
+            loop(0, GROUPS, lambda g: relay_copy(g).wait_recv())
+        project(plane(2))
         width = NE * 8
         gate, up, back = pre[:, :width], pre[:, width : 2 * width], pre[:, 2 * width :]
         s = jax.nn.sigmoid(gate)
@@ -424,50 +433,70 @@
                 rs.at[n, t].reshape(8 * PER, COLS)[:, cols] = moved.astype(BF)
         if n == 0:
             own_result.start()
+            left(ws.at[:, pl.ds(0, NE - 1)], t_send.at[0])
             loop(1, PER, lambda i: return_copy(i).start())
         else:
             loop(n * PER, (n + 1) * PER, lambda i: return_copy(i).start())
 
-    def result_forward(g):
-        group = hr.at[core, :, pl.ds(g * GROUP, GROUP)]
+    def result_group(g, count):
+        per = PER // GROUP
+        return hr.at[core, g // per, :, pl.ds(lax.rem(g, per) * GROUP, count)]
+
+    def result_forward(group, n):
         return pltpu.make_async_remote_copy(
             src_ref=group,
             dst_ref=group,
             send_sem=rf_send.at[0],
-            recv_sem=rf_recv.at[0],
+            recv_sem=rf_recv.at[n],
             device_id=partner,
             device_id_type=MESH,
         )
 
     def result_step(g):
-        landed(hr.at[core, :, pl.ds(g * GROUP, GROUP)], r_recv.at[g])
-        result_forward(g).start()
+        group = result_group(g, GROUP)
+        landed(group, r_recv.at[g])
+        result_forward(group, g // (PER // GROUP)).start()
 
     own_result.wait()
-    landed(hr.at[core, :, pl.ds(1, GROUP - 1)], r_recv.at[0])
-    result_forward(0).start()
-    loop(1, GROUPS, result_step)
+    landed(hr.at[core, 0, :, pl.ds(1, GROUP - 1)], r_recv.at[0])
+    result_forward(result_group(0, GROUP), 0).start()
+    loop(1, PER // GROUP, result_step)
+    landed(hr.at[1 - core, 0], rf_recv.at[0])
+
+    def settle(b):
+        half, h = b // 2, lax.rem(b, 2)
+        source = hr.at[half, 0, pl.ds(h, 2)].reshape(2 * 8 * PER, COLS)
+        for c in range(COLS // STEP):
+            cols = slice(c * STEP, (c + 1) * STEP)
+            part_out[b, :, cols] = dot(table[0, h], source[:, cols]).astype(BF)
+
+    loop(0, 4, settle)
+    loop(PER // GROUP, GROUPS - 1, result_step)
+    for i in range(GROUP):
+        piece = hr.at[core, CHUNKS - 1, :, pl.ds(PER - GROUP + i, 1)]
+        landed(piece, r_recv.at[GROUPS - 1 + i])
+        result_forward(piece, CHUNKS - 1).start()
 
     left(ws.at[:, pl.ds(0, NE - 1)], w_send.at[0])
-    left(ts.at[:, pl.ds(0, NE - 1)], t_send.at[0])
-    left(hr.at[core, :, pl.ds(0, NE - 1)], r_send.at[0])
+    left(ws.at[:, pl.ds(0, NE - 1)], r_send.at[0])
     left(wr.at[pl.ds(0, 3)], y_send.at[0])
     left(tr.at[core], tf_send.at[0])
     for n in range(CHUNKS):
         for h in range(2):
             left(ps.at[n, h], p_send.at[n, h])
     left(hr.at[core], rf_send.at[0])
-    landed(hr.at[1 - core], rf_recv.at[0])
-
-
-def finish(hr, table, out_ref, grad_ref):
+    landed(hr.at[1 - core, CHUNKS - 1], rf_recv.at[CHUNKS - 1])
+
+
+def finish(hr, table, part_out, out_ref, grad_ref):
     b = pl.program_id(0)
     half, h = b // 2, lax.rem(b, 2)
     n_tok = out_ref.shape[0]
-    source = hr.at[half, pl.ds(h, 2)].reshape(2 * NE * 8, COLS)
+    last = CHUNKS - 1
+    source = hr.at[half, last, pl.ds(h, 2)].reshape(2 * 8 * PER, COLS)
     for c in range(COLS // STEP):
         cols = slice(c * STEP, (c + 1) * STEP)
-        value = dot(table[h], source[:, cols]).astype(BF)
+        value = (dot(table[last, h], source[:, cols]) + part_out[b, :, cols].astype(F32)).astype(BF)
         out_ref[:, cols] = value[:n_tok]
         grad_ref[:, cols] = value[n_tok:]
 
@@ -478,14 +507,15 @@
     dma = pltpu.SemaphoreType.DMA
     rows = CAP * PER
     vmem = pl.BlockSpec(memory_space=pltpu.VMEM)
-    results, table = pl.pallas_call(
+    results, table, settled = pl.pallas_call(
         kernel,
         out_shape=(
-            pltpu.VMEM((2, TILES, NE, 8, COLS), BF),
-            pltpu.VMEM((2, 2 * n_tok, 2 * NE * 8), BF),
+            pltpu.VMEM((2, CHUNKS, TILES, PER, 8, COLS), BF),
+            pltpu.VMEM((CHUNKS, 2, 2 * n_tok, 2 * 8 * PER), BF),
+            pltpu.VMEM((4, 2 * n_tok, COLS), BF),
         ),
         in_specs=[pl.BlockSpec(memory_space=pltpu.HBM)] * 7,
-        out_specs=(vmem, vmem),
+        out_specs=(vmem, vmem, vmem),
         scratch_shapes=[
             pltpu.VMEM((n_tok, width), BF),
             pltpu.VMEM((n_tok, width), BF),
@@ -519,9 +549,9 @@
             dma((CHUNKS, 2)),
             dma((CHUNKS, 2)),
             dma((1,)),
-            dma((GROUPS,)),
+            dma((GROUPS - 1 + GROUP,)),
             dma((1,)),
-            dma((1,)),
+            dma((CHUNKS,)),
         ],
         compiler_params=pltpu.CompilerParams(
             collective_id=0, has_side_effects=True, vmem_limit_bytes=VMEM_BYTES
@@ -533,10 +563,10 @@
         finish,
         grid=(width // COLS,),
         out_shape=(shape, shape),
-        in_specs=[vmem, vmem],
+        in_specs=[vmem, vmem, vmem],
         out_specs=(column, column),
         compiler_params=pltpu.CompilerParams(vmem_limit_bytes=16 << 20),
-    )(results, table)
+    )(results, table, settled)
 
 
 def solution(mesh):

time: 121 us -> 119 us (0.983)
  no operation moved by 1% of the time
where the time goes in v3:
time: 119 us
  Pallas kernels  119 us (100%)
    pallas_call x1, Pallas kernels, per_device(): pl.pallas_call(kernel, out_shape=(pltpu.VMEM((2, CHUNKS, TILES, PER, 8, C...  116 us
    pallas_call x1, Pallas kernels, per_device(): pl.pallas_call(finish, grid=(width // COLS,), out_shape=(shape, shape), i...  2.48 us

profile of v3, /device:TPU:1, one launch (start us, length us, event | category | flops | bytes accessed | tf_op | source)
XLA Modules:
  0.0 119.3 jit_solution(6458702724544319265)
XLA Ops:
  0.6 116.2 %shard_map.86 = (bf16[2,2,3,16,8,1024]{5,4,3,2,1,0:T(8,128)(2,1)S(1)}, bf16[2,2,256,256]{3,2,1,0:T(8,128)(2,1)S(1)}, bf16[4,256,1024]{2,1,0:T(8,128)(2,1)S(1)}) custom-call(bf16[128,4096]{1,0:T(8,128)(2,1)} %tok_hbm.1, bf16[128,4096]{1,0:T(8,128)(2,1)} %cot_hbm.1, s32[1,128]{1,0:T(1,128)} %bitcast.1, s32[32,512]{1,0:T(8,128)} %cluster_hbm.1, ...), custom_call_target="tpu_custom_call" | custom-call | tf_op jit(solution)/shard_map/pallas_call | solution.py:510
  116.8 2.5 %shard_map.87 = (bf16[128,4096]{1,0:T(8,128)(2,1)}, bf16[128,4096]{1,0:T(8,128)(2,1)}) custom-call(bf16[2,2,3,16,8,1024]{5,4,3,2,1,0:T(8,128)(2,1)S(1)} %get-tuple-element.5.hr, bf16[2,2,256,256]{3,2,1,0:T(8,128)(2,1)S(1)} %get-tuple-element.6.table, bf16[4,256,1024]{2,1,0:T(8,128)(2,1)S(1)} %get-tuple-element.7.part_out), custom_call_target="tpu_custom_call" | custom-call | tf_op jit(solution)/shard_map/pallas_call | solution.py:562

commit v4 on v3

--- a/solution.py
+++ b/solution.py
@@ -488,17 +488,26 @@
     landed(hr.at[1 - core, CHUNKS - 1], rf_recv.at[CHUNKS - 1])
 
 
-def finish(hr, table, part_out, out_ref, grad_ref):
-    b = pl.program_id(0)
-    half, h = b // 2, lax.rem(b, 2)
-    n_tok = out_ref.shape[0]
+def finish(hr, table, part_out, out_hbm, grad_hbm, out_buf, grad_buf, sem):
+    n_tok = out_buf.shape[0]
     last = CHUNKS - 1
-    source = hr.at[half, last, pl.ds(h, 2)].reshape(2 * 8 * PER, COLS)
-    for c in range(COLS // STEP):
-        cols = slice(c * STEP, (c + 1) * STEP)
-        value = (dot(table[last, h], source[:, cols]) + part_out[b, :, cols].astype(F32)).astype(BF)
-        out_ref[:, cols] = value[:n_tok]
-        grad_ref[:, cols] = value[n_tok:]
+    copies = []
+    for b in range(4):
+        half, h = b // 2, b % 2
+        source = hr.at[half, last, pl.ds(h, 2)].reshape(2 * 8 * PER, COLS)
+        for c in range(COLS // STEP):
+            cols = slice(c * STEP, (c + 1) * STEP)
+            total = dot(table[last, h], source[:, cols]) + part_out[b, :, cols].astype(F32)
+            value = total.astype(BF)
+            at = slice(b * COLS + c * STEP, b * COLS + (c + 1) * STEP)
+            out_buf[:, at] = value[:n_tok]
+            grad_buf[:, at] = value[n_tok:]
+            for k, (buf, hbm) in enumerate(((out_buf, out_hbm), (grad_buf, grad_hbm))):
+                copy = pltpu.make_async_copy(buf.at[:, at], hbm.at[:, at], sem.at[len(copies)])
+                copy.start()
+                copies.append(copy)
+    for copy in copies:
+        copy.wait()
 
 
 def per_device(tokens, cotangent, routes, cluster, w_gate, w_up, w_down):
@@ -557,14 +566,18 @@
             collective_id=0, has_side_effects=True, vmem_limit_bytes=VMEM_BYTES
         ),
     )(tokens, cotangent, routes.reshape(1, n_tok), cluster, w_gate, w_up, w_down)
-    column = pl.BlockSpec((n_tok, COLS), lambda b: (0, b))
     shape = jax.ShapeDtypeStruct((n_tok, width), BF)
+    hbm = pl.BlockSpec(memory_space=pltpu.HBM)
     return pl.pallas_call(
         finish,
-        grid=(width // COLS,),
         out_shape=(shape, shape),
         in_specs=[vmem, vmem, vmem],
-        out_specs=(column, column),
+        out_specs=(hbm, hbm),
+        scratch_shapes=[
+            pltpu.VMEM((n_tok, width), BF),
+            pltpu.VMEM((n_tok, width), BF),
+            dma((2 * width // STEP,)),
+        ],
         compiler_params=pltpu.CompilerParams(vmem_limit_bytes=16 << 20),
     )(results, table, settled)
 

time: 119 us -> 119 us (level)
  no operation moved by 1% of the time
where the time goes in v4:
time: 119 us; the launch traced here: 118 us
  Pallas kernels  118 us (99%)
    pallas_call x1, Pallas kernels, per_device(): pl.pallas_call(kernel, out_shape=(pltpu.VMEM((2, CHUNKS, TILES, PER, 8, C...  116 us

profile of v4, /device:TPU:1, one launch (start us, length us, event | category | flops | bytes accessed | tf_op | source)
XLA Modules:
  0.0 118.5 jit_solution(7335829195989938471)
XLA Ops:
  0.6 116.2 %shard_map.86 = (bf16[2,2,3,16,8,1024]{5,4,3,2,1,0:T(8,128)(2,1)S(1)}, bf16[2,2,256,256]{3,2,1,0:T(8,128)(2,1)S(1)}, bf16[4,256,1024]{2,1,0:T(8,128)(2,1)S(1)}) custom-call(bf16[128,4096]{1,0:T(8,128)(2,1)} %tok_hbm.1, bf16[128,4096]{1,0:T(8,128)(2,1)} %cot_hbm.1, s32[1,128]{1,0:T(1,128)} %bitcast.1, s32[32,512]{1,0:T(8,128)} %cluster_hbm.1, ...), custom_call_target="tpu_custom_call" | custom-call | tf_op jit(solution)/shard_map/pallas_call | solution.py:519
  116.8 1.6 %shard_map.87 = (bf16[128,4096]{1,0:T(8,128)(2,1)}, bf16[128,4096]{1,0:T(8,128)(2,1)}) custom-call(bf16[2,2,3,16,8,1024]{5,4,3,2,1,0:T(8,128)(2,1)S(1)} %get-tuple-element.5.hr, bf16[2,2,256,256]{3,2,1,0:T(8,128)(2,1)S(1)} %get-tuple-element.6.table, bf16[4,256,1024]{2,1,0:T(8,128)(2,1)S(1)} %get-tuple-element.7.part_out), custom_call_target="tpu_custom_call" | custom-call | tf_op jit(solution)/shard_map/pallas_call | solution.py:571
